TPU v7x, 128 devices: a whole 4x4x4 slice. The times are simulated.
128 devices in a mesh: tm: 8 (over z, x_hi), docs: 16 (over y, x_lo, core).
Axes of the slice: x: 4 (x_hi: 2, x_lo: 2; x = x_hi * 2 + x_lo), y: 4, z: 4, core: 2. Of those that a mesh axis runs over, the one named last changes fastest.
Arguments:
- counts: int32 [8, 1024, 32768], P('tm', 'docs'), may hold values from 0 to 5, as said below
- topic_means: float32 [8, 32768, 128], P('tm', 'docs'), may hold values from -80 to 170
- doc_topics_init: float32 [8, 1024, 128], P('tm', 'docs'), may hold values from 0.5 to 20
- dirichlet_prior: float32 [128], replicated, may hold values from 0.05 to 1
- chain_var: float32 [128], replicated, may hold values from 0.005 to 0.5
- obs_noise: float32 [128], replicated, may hold values from 0.1 to 10
Outputs:
- smoothed_means: float32 [8, 32768, 128], P('tm', 'docs')
- doc_topics: float32 [8, 1024, 128], P('tm', 'docs')
Inputs may be any that keep to these rules, and one draw needn't show every extreme that they name: `counts`: each entry is 0 or a count of 1 to 5; each word has its own share of nonzero entries, between a quarter and three quarters.
All inputs are finite; a program needn't handle non-finite values.
Results may differ from a plain program's by a relative error of at most 0.01.
Values may be sent and summed in bfloat16 or wider, within the bound.
No kernel may reach another device: no remote copies, remote signals or barrier semaphores. Data moves between devices by JAX's collectives and lax.ppermute only.
A program may use at most 128 MiB of HBM per device.

v0:
```python
import jax
import jax.numpy as jnp
from jax import lax
from jax.sharding import Mesh
from jax.sharding import PartitionSpec as P

V = 32768
ITERS_E = 4
TM = ("tm_0", "tm_1")
TM_DOCS = ("tm_0", "tm_1", "docs")
prior_count = 0.5
initial_scale = 1000.0


def merged(part, axis, combine):
    gathered = jax.tree.map(lambda a: lax.all_gather(a, axis), part)

    def take(source):
        return jax.tree.map(lambda a: lax.dynamic_index_in_dim(a, source, 0, False), gathered)

    return lax.fori_loop(
        1, lax.axis_size(axis), lambda source, state: combine(state, take(source)), take(0)
    )


def filled_with(shard, identity):
    return jax.tree.map(
        lambda a, e: jnp.broadcast_to(jnp.asarray(e, a.dtype), a.shape), shard, identity
    )


def carried_in(shard, axes, combine, identity):
    before = start = filled_with(shard, identity)
    subtotal = shard
    for axis in reversed(axes):
        devices, place = (lax.axis_size(axis), lax.axis_index(axis))
        pieces = jax.tree.map(
            lambda part, kind: lax.all_gather(part.astype(kind), axis),
            subtotal,
            (jnp.bfloat16, jnp.bfloat16),
        )
        inside, subtotal = (start, start)
        for k in range(devices):
            passed = k < place
            subtotal = combine(
                subtotal, jax.tree.map(lambda part, own: part[k].astype(own.dtype), pieces, shard)
            )
            inside = jax.tree.map(lambda new, old: jnp.where(passed, new, old), subtotal, inside)
        before = combine(inside, before)
    return before


def prefix_by_axis(shard, axes, combine, identity):
    before = start = filled_with(shard, identity)
    subtotal = shard
    for axis in reversed(axes):
        devices, place = (lax.axis_size(axis), lax.axis_index(axis))
        pieces = jax.tree.map(
            lambda part, kind: lax.all_gather(part.astype(kind), axis),
            subtotal,
            jax.tree.map(lambda a: jnp.bfloat16 if a.dtype == jnp.float32 else a.dtype, shard),
        )
        inside, subtotal = (start, start)
        for k in reversed(range(devices)):
            passed = k > place
            subtotal = combine(
                subtotal, jax.tree.map(lambda part, own: part[k].astype(own.dtype), pieces, shard)
            )
            inside = jax.tree.map(lambda new, old: jnp.where(passed, new, old), subtotal, inside)
        before = combine(inside, before)
    return before


def chain_factors(totals, chain_var, obs_noise):
    relative = jnp.sum(totals, axis=1, keepdims=True) / (totals.shape[1] * totals)
    noise = obs_noise[None, :] * relative

    def advance(previous, noise_level):
        predicted = previous + chain_var
        own_gain = predicted / (predicted + noise_level)
        current = (1.0 - own_gain) * predicted
        return (current, (own_gain, current))

    unused, (gains, filtered_var) = lax.scan(advance, initial_scale * chain_var, noise)
    smooth = filtered_var / (filtered_var + chain_var)
    smooth = jnp.concatenate([smooth[:-1], jnp.zeros_like(smooth[-1:])], axis=0)
    return (gains, smooth)


def compose(former, latter):
    return (former[0] * latter[0], latter[0] * former[1] + latter[1])


def join_mass(former, latter):
    highest = jnp.maximum(former[0], latter[0])
    return (
        highest,
        former[1] * jnp.exp(former[0] - highest) + latter[1] * jnp.exp(latter[0] - highest),
    )


def body(counts, topic_means, doc_topics_init, dirichlet_prior, chain_var, obs_noise):
    topic_slab = topic_means[0]
    concentration = doc_topics_init[0]
    count_wide = counts[0].astype(jnp.float32)
    local_peak = jnp.max(topic_slab, axis=0)
    local_mass = jnp.sum(jnp.exp(topic_slab - local_peak[None, :]), axis=0)
    column_peak, column_mass = merged((local_peak, local_mass), "docs", join_mass)
    beta_slab = jnp.exp(topic_slab - (column_peak + jnp.log(column_mass))[None, :]).astype(
        jnp.bfloat16
    )
    beta_full = lax.all_gather(beta_slab, "docs", axis=0, tiled=True)
    for sweep_index in range(ITERS_E):
        proportions = jnp.exp(lax.digamma(concentration)).astype(jnp.bfloat16)
        mixture = lax.dot_general(
            proportions, beta_full, (((1,), (1,)), ((), ())), preferred_element_type=jnp.float32
        )
        ratios = (count_wide / mixture).astype(jnp.bfloat16)
        update = proportions.astype(jnp.float32) * jnp.dot(
            ratios, beta_full, preferred_element_type=jnp.float32
        )
        concentration = dirichlet_prior[None, :] + update
    word_stats = lax.psum_scatter(
        (
            beta_full.astype(jnp.float32)
            * lax.dot_general(
                ratios, proportions, (((0,), (0,)), ((), ())), preferred_element_type=jnp.float32
            )
        ).astype(jnp.bfloat16),
        "docs",
        scatter_dimension=0,
        tiled=True,
    ).astype(jnp.float32)
    slice_index = lax.axis_index(TM)
    slices = lax.axis_size(TM)
    own_row = (jnp.arange(slices) == slice_index).astype(jnp.float32)
    placed = own_row[:, None] * jnp.sum(update, axis=0)[None, :]
    totals = lax.psum(placed, TM_DOCS)
    gains, smooth = chain_factors(totals, chain_var, obs_noise)
    own_total = jnp.sum(own_row[:, None] * totals, axis=0)
    own_gain = jnp.sum(own_row[:, None] * gains, axis=0)
    own_factor = jnp.sum(own_row[:, None] * smooth, axis=0)
    pseudo = jnp.log(word_stats + prior_count) - jnp.log((own_total + prior_count * V) / V)[None, :]
    forward_rate = 1.0 - own_gain
    forward_term = own_gain[None, :] * pseudo
    neutral = (jnp.ones_like(forward_rate), jnp.zeros_like(forward_term))
    entering = carried_in((forward_rate, forward_term), TM, compose, neutral)[1]
    filtered = forward_rate[None, :] * entering + forward_term
    back_term = (1.0 - own_factor)[None, :] * filtered
    following = prefix_by_axis((own_factor, back_term), TM, compose, neutral)[1]
    smoothed = own_factor[None, :] * following + back_term
    return (smoothed[None], concentration[None])


def solution(mesh):
    split = Mesh(mesh.devices.reshape(4, 2, mesh.shape["docs"]), ("tm_0", "tm_1", "docs"))
    placed = (P(TM, "docs", None), P(TM, "docs", None), P(TM, "docs", None), P(), P(), P())
    return jax.shard_map(
        body,
        mesh=split,
        in_specs=placed,
        out_specs=(P(TM, "docs", None), P(TM, "docs", None)),
        check_vma=False,
    )
```

profile of v0, /device:TPU:1, one launch (start us, length us, event | category | flops | bytes accessed | tf_op | source)
XLA Modules:
  0.0 390.9 jit_solution(17476896300496999206)
XLA Ops:
  7.2 0.0 all-gather.18.cloned.1.call-start
  7.2 1.5 reduce_max.9
  8.7 1.5 fusion.51
  10.2 21.2 %all-gather.7 = f32[16,1,128]{2,1,0:T(1,128)S(1)} all-gather(f32[1,1,128]{2,1,0:T(1,128)S(1)} %bitcast.319), channel_id=3, replica_groups=mesh['tm_0'=4,'tm_1'=2,'docs'=16] {'docs'}, dimensions={0}, use_global_device_ids=true | all-gather | bytes 8704 | tf_op jit(solution)/shard_map/all_gather | solution.py:16
  31.4 16.3 %all-gather.6 = f32[16,1,128]{2,1,0:T(1,128)S(1)} all-gather(f32[1,1,128]{2,1,0:T(1,128)S(1)} %bitcast.318), channel_id=2, replica_groups=mesh['tm_0'=4,'tm_1'=2,'docs'=16] {'docs'}, dimensions={0}, use_global_device_ids=true | all-gather | bytes 8704 | tf_op jit(solution)/shard_map/all_gather | solution.py:16
  47.7 0.7 while.33
  48.4 2.2 fusion.53
  50.5 0.0 all-gather.18.cloned.1.call-update
  50.6 0.0 copy-start.2
  50.6 0.0 reduce-scatter.2.cloned.1.call-start
  50.6 51.7 %all-gather.18.cloned.1.call-done = bf16[32768,128]{1,0:T(8,128)(2,1)} async-done(((bf16[2048,128]{1,0:T(8,128)(2,1)}), bf16[32768,128]{1,0:T(8,128)(2,1)}) %all-gather.18.cloned.1.call-update) | async-done | bytes 8388624 | tf_op jit(solution)/shard_map/all_gather | solution.py:112
  102.3 13.1 %fusion.62 = bf16[64,128]{1,0:T(8,128)(2,1)S(1)} fusion(bf16[32768,128]{1,0:T(8,128)(2,1)} %all-gather.18.cloned.1.call-done, s32[1,64,32768]{2,1,0:T(8,128)} %param.10, f32[1,64,128]{2,1,0:T(8,128)} %param.12, f32[128]{0:T(128)} %param.13), kind=kOutput, calls=%fused_computation.109 | convolution fusion | flops 1081925632 | bytes 16826880 | tf_op jit(solution)/shard_map/dot_general | solution.py:119
  115.4 0.0 copy-done.2
  115.4 12.6 %fusion.66 = bf16[64,128]{1,0:T(8,128)(2,1)S(1)} fusion(bf16[32768,128]{1,0:T(8,128)(2,1)} %all-gather.18.cloned.1.call-done, bf16[64,128]{1,0:T(8,128)(2,1)S(1)} %fusion.62, s32[1,64,32768]{2,1,0:T(8,128)} %param.10, f32[128]{0:T(128)S(1)} %copy-done.2), kind=kOutput, calls=%fused_computation.113 | convolution fusion | flops 1080680448 | bytes 16810496 | tf_op jit(solution)/shard_map/dot_general | solution.py:119
  128.0 12.4 %fusion.15 = f32[64,128]{1,0:T(8,128)S(1)} fusion(bf16[32768,128]{1,0:T(8,128)(2,1)} %all-gather.18.cloned.1.call-done, bf16[64,128]{1,0:T(8,128)(2,1)S(1)} %fusion.66, s32[1,64,32768]{2,1,0:T(8,128)} %param.10, f32[128]{0:T(128)S(1)} %copy-done.2), kind=kOutput, calls=%fused_computation.35 | convolution fusion | flops 1080057856 | bytes 16826880 | tf_op jit(solution)/shard_map/dot_general | solution.py:119
  140.4 9.2 %fusion.3 = bf16[64,32768]{1,0:T(8,128)(2,1)S(1)} fusion(bf16[32768,128]{1,0:T(8,128)(2,1)} %all-gather.18.cloned.1.call-done, s32[1,64,32768]{2,1,0:T(8,128)} %param.10, f32[64,128]{1,0:T(8,128)S(1)} %fusion.15), kind=kOutput, calls=%fused_computation.11 | convolution fusion | flops 543784960 | bytes 21004288 | tf_op jit(solution)/shard_map/dot_general | solution.py:115
  149.6 0.0 copy-start
  149.6 1.9 copy-done
  151.5 7.3 %fusion.2 = bf16[32768,128]{1,0:T(8,128)(2,1)} fusion(bf16[64,32768]{1,0:T(8,128)(2,1)S(1)} %fusion.3, bf16[32768,128]{1,0:T(8,128)(2,1)} %all-gather.18.cloned.1.call-done, f32[64,128]{1,0:T(8,128)S(1)} %fusion.15), kind=kOutput, calls=%fused_computation.9 | convolution fusion | flops 550076416 | bytes 21004288 | tf_op jit(solution)/shard_map/dot_general | solution.py:126
  158.8 0.0 copy-start.1
  158.8 0.0 reduce-scatter.2.cloned.1.call-update
  158.9 0.0 all-gather.24.cloned.1.call-start
  158.9 0.5 copy-done.1
  159.5 0.0 copy-start.3
  159.5 0.0 copy-start.4
  159.5 7.0 %add_bitcast_fusion = (f32[1,64,128]{2,1,0:T(8,128)}, f32[128]{0:T(128)S(1)}) fusion(f32[128]{0:T(128)S(1)} %copy-done.2, bf16[64,32768]{1,0:T(8,128)(2,1)} %copy-done, bf16[32768,128]{1,0:T(8,128)(2,1)} %all-gather.18.cloned.1.call-done, f32[64,128]{1,0:T(8,128)S(1)} %fusion.15), kind=kOutput, calls=%fused_computation.129 | convolution fusion | flops 537526144 | bytes 12649472 | tf_op jit(solution)/shard_map/dot_general | solution.py:119
  166.5 0.1 broadcast_multiply_fusion
  166.6 67.0 %psum.7 = f32[8,128]{1,0:T(8,128)S(1)} all-reduce(f32[8,128]{1,0:T(8,128)S(1)} %broadcast_multiply_fusion), channel_id=1, replica_groups=mesh['tm_0'=4,'tm_1'=2,'docs'=16] {'tm_0','tm_1','docs'}, use_global_device_ids=true, to_apply=%region_5.6 | all-reduce | flops 1024 | bytes 8192 | tf_op jit(solution)/shard_map/psum | solution.py:138
  233.6 0.1 multiply_reduce_fusion
  233.7 0.0 copy-done.3
  233.7 0.1 divide_multiply_fusion
  233.8 0.9 while.34
  234.7 0.0 copy-done.4
  234.7 0.1 fusion.192
  234.8 22.3 %reduce-scatter.2.cloned.1.call-done = bf16[2048,128]{1,0:T(8,128)(2,1)} async-done(((bf16[32768,128]{1,0:T(8,128)(2,1)}), bf16[2048,128]{1,0:T(8,128)(2,1)}) %reduce-scatter.2.cloned.1.call-update) | async-done | bytes 524304 | tf_op jit(solution)/shard_map/reduce_scatter | solution.py:123
  257.1 2.1 fusion.54
  259.2 0.0 all-gather.24.cloned.1.call-update
  259.2 0.0 all-gather.20.cloned.1.call-start
  259.3 4.6 %all-gather.10 = bf16[2,1,128]{2,1,0:T(2,128)(2,1)S(1)} all-gather(bf16[1,1,128]{2,1,0:T(2,128)(2,1)S(1)} %get-tuple-element.221), channel_id=5, replica_groups=mesh['tm_0'=4,'tm_1'=2,'docs'=16] {'tm_1'}, dimensions={0}, use_global_device_ids=true | all-gather | bytes 768 | tf_op jit(solution)/shard_map/all_gather | solution.py:38
  263.9 21.5 %all-gather.24.cloned.1.call-done = bf16[4096,128]{1,0:T(8,128)(2,1)} async-done(((bf16[2048,128]{1,0:T(8,128)(2,1)}), bf16[4096,128]{1,0:T(8,128)(2,1)}) %all-gather.24.cloned.1.call-update) | async-done | bytes 1048592 | tf_op jit(solution)/shard_map/all_gather | solution.py:38
  285.4 2.2 fusion.33
  287.6 0.0 all-gather.20.cloned.1.call-update
  287.6 0.0 all-gather.26.cloned.1.call-start
  287.7 7.9 %all-gather.11 = bf16[4,1,128]{2,1,0:T(2,128)(2,1)S(1)} all-gather(bf16[1,1,128]{2,1,0:T(2,128)(2,1)S(1)} %get-tuple-element.216), channel_id=1, replica_groups=mesh['tm_0'=4,'tm_1'=2,'docs'=16] {'tm_0'}, dimensions={0}, use_global_device_ids=true | all-gather | bytes 1280 | tf_op jit(solution)/shard_map/all_gather | solution.py:38
  295.6 22.6 %all-gather.20.cloned.1.call-done = bf16[4,2048,128]{2,1,0:T(8,128)(2,1)} async-done(((bf16[1,2048,128]{2,1,0:T(8,128)(2,1)}), bf16[4,2048,128]{2,1,0:T(8,128)(2,1)}) %all-gather.20.cloned.1.call-update) | async-done | bytes 2097168 | tf_op jit(solution)/shard_map/all_gather | solution.py:38
  318.2 3.9 %fusion.309 = (bf16[2048,128]{1,0:T(8,128)(2,1)}, f32[2048,128]{1,0:T(8,128)S(1)}) fusion(f32[128]{0:T(128)S(1)} %multiply_log_fusion, bf16[2048,128]{1,0:T(8,128)(2,1)} %reduce-scatter.2.cloned.1.call-done, f32[128]{0:T(128)S(1)} %get-tuple-element.175, pred[]{:T(512)S(6)} %gt.19, bf16[4096,128]{1,0:T(8,128)(2,1)} %all-gather.24.cloned.1.call-done, ...), kind=kLoop, calls=%fused_computation.345 | loop fusion | flops 8388608 | bytes 5248518 | tf_op jit(solution)/shard_map/convert_element_type | solution.py:59
  322.2 0.0 all-gather.26.cloned.1.call-update
  322.2 0.0 all-gather.22.cloned.1.call-start
  322.2 4.6 %all-gather.8 = bf16[2,1,128]{2,1,0:T(2,128)(2,1)S(1)} all-gather(bf16[1,1,128]{2,1,0:T(2,128)(2,1)S(1)} %get-tuple-element.218), channel_id=4, replica_groups=mesh['tm_0'=4,'tm_1'=2,'docs'=16] {'tm_1'}, dimensions={0}, use_global_device_ids=true | all-gather | bytes 768 | tf_op jit(solution)/shard_map/all_gather | solution.py:59
  326.8 20.7 %all-gather.26.cloned.1.call-done = bf16[4096,128]{1,0:T(8,128)(2,1)} async-done(((bf16[2048,128]{1,0:T(8,128)(2,1)}), bf16[4096,128]{1,0:T(8,128)(2,1)}) %all-gather.26.cloned.1.call-update) | async-done | bytes 1048592 | tf_op jit(solution)/shard_map/all_gather | solution.py:59
  347.5 2.2 fusion.37
  349.7 0.0 all-gather.22.cloned.1.call-update
  349.7 7.9 %all-gather.9 = bf16[4,1,128]{2,1,0:T(2,128)(2,1)S(1)} all-gather(bf16[1,1,128]{2,1,0:T(2,128)(2,1)S(1)} %get-tuple-element.212), channel_id=1, replica_groups=mesh['tm_0'=4,'tm_1'=2,'docs'=16] {'tm_0'}, dimensions={0}, use_global_device_ids=true | all-gather | bytes 1280 | tf_op jit(solution)/shard_map/all_gather | solution.py:59
  357.6 22.7 %all-gather.22.cloned.1.call-done = bf16[4,2048,128]{2,1,0:T(8,128)(2,1)} async-done(((bf16[1,2048,128]{2,1,0:T(8,128)(2,1)}), bf16[4,2048,128]{2,1,0:T(8,128)(2,1)}) %all-gather.22.cloned.1.call-update) | async-done | bytes 2097168 | tf_op jit(solution)/shard_map/all_gather | solution.py:59
  380.3 3.7 fusion.24
  (57 shorter events, 1.2 us)
Async XLA Ops:
  7.2 95.1 %all-gather.18.cloned.1.call-start = ((), (), s32[]{:S(2)}) async-start(), calls=%async_computation.1 | async-start | bytes 8912896 | tf_op jit(solution)/shard_map/all_gather | solution.py:112
  50.6 64.9 %copy-start.2 = (f32[128]{0:T(128)S(1)}, f32[128]{0:T(128)}, u32[]{:S(2)}) copy-start(f32[128]{0:T(128)} %param.13) | copy-start | bytes 1540
  50.6 206.5 %reduce-scatter.2.cloned.1.call-start = ((), (), s32[]{:S(2)}) async-start(), calls=%async_computation.2 | async-start | bytes 8912896 | tf_op jit(solution)/shard_map/reduce_scatter | solution.py:123
  149.6 1.9 copy-start
  158.8 0.7 copy-start.1
  158.9 126.5 %all-gather.24.cloned.1.call-start = ((), (), s32[]{:S(2)}) async-start(), calls=%async_computation.5 | async-start | bytes 1572864 | tf_op jit(solution)/shard_map/all_gather | solution.py:38
  159.5 74.2 %copy-start.3 = (f32[128]{0:T(128)S(1)}, f32[128]{0:T(128)}, u32[]{:S(2)}) copy-start(f32[128]{0:T(128)} %param.15) | copy-start | bytes 1540
  159.5 75.2 %copy-start.4 = (pred[8]{0:T(512)(128)(4,1)S(1)}, pred[8]{0:T(512)(128)(4,1)}, u32[]{:S(2)}) copy-start(pred[8]{0:T(512)(128)(4,1)} %constant.117.clone.1) | copy-start | bytes 28
  259.2 59.0 %all-gather.20.cloned.1.call-start = ((), (), s32[]{:S(2)}) async-start(), calls=%async_computation.3 | async-start | bytes 2621440 | tf_op jit(solution)/shard_map/all_gather | solution.py:38
  287.6 59.9 %all-gather.26.cloned.1.call-start = ((), (), s32[]{:S(2)}) async-start(), calls=%async_computation.6 | async-start | bytes 1572864 | tf_op jit(solution)/shard_map/all_gather | solution.py:59
  322.2 58.1 %all-gather.22.cloned.1.call-start = ((), (), s32[]{:S(2)}) async-start(), calls=%async_computation.4 | async-start | bytes 2621440 | tf_op jit(solution)/shard_map/all_gather | solution.py:59
Sparse Core Ops, SparseCore 0:
  50.7 51.5 all-gather.17
  159.0 98.0 reduce-scatter.1
  259.3 26.0 all-gather.23
  287.7 30.4 all-gather.19
  322.3 25.1 all-gather.25
  349.8 30.4 all-gather.21
where the time goes:
time: 391 us
  waiting for transfers between devices  162 us (41%)
  blocking collectives  129 us (33%)
  matrix products  61.6 us (16%)
  other arithmetic  20.3 us (5%)
  between operations  14.3 us (4%)
    psum x1, blocking collectives, body(): totals = lax.psum(placed, TM_DOCS)  67 us
    all_gather x1, waiting for transfers between devices, body(): beta_full = lax.all_gather(beta_slab, 'docs', axis=0, tiled=True)  51.7 us
    dot_general x4, matrix products, body(): jnp.dot(ratios, beta_full, preferred_element_type=jnp.float32)  45.1 us
    all_gather x2, waiting for transfers between devices, carried_in(): lax.all_gather(part.astype(kind), axis)  44.2 us
    all_gather x2, waiting for transfers between devices, prefix_by_axis(): lax.all_gather(part.astype(kind), axis)  43.4 us
    all_gather x2, blocking collectives, merged(): gathered = jax.tree.map(lambda a: lax.all_gather(a, axis), part)  37.5 us
    reduce_scatter x1, waiting for transfers between devices, body(): lax.psum_scatter((beta_full.astype(jnp.float32) * lax.dot_general(ratios,...  22.3 us
    all_gather x2, blocking collectives, carried_in(): lax.all_gather(part.astype(kind), axis)  12.5 us
  transfers between devices with their start and end apart: 6, of which 6 were waited for; matrix products, arithmetic and copies ran while one was open for 2% of the time, Pallas kernels for 0%

commit v1 on v0

--- a/solution.py
+++ b/solution.py
@@ -3,6 +3,7 @@
 from jax import lax
 from jax.sharding import Mesh
 from jax.sharding import PartitionSpec as P
+from jax.lax import all_gather
 
 V = 32768
 ITERS_E = 4
@@ -135,7 +136,8 @@
     slices = lax.axis_size(TM)
     own_row = (jnp.arange(slices) == slice_index).astype(jnp.float32)
     placed = own_row[:, None] * jnp.sum(update, axis=0)[None, :]
-    totals = lax.psum(placed, TM_DOCS)
+    switch_the_indices = lambda point: all_gather(point, TM_DOCS).sum(axis=0)
+    totals = switch_the_indices(placed)
     gains, smooth = chain_factors(totals, chain_var, obs_noise)
     own_total = jnp.sum(own_row[:, None] * totals, axis=0)
     own_gain = jnp.sum(own_row[:, None] * gains, axis=0)

time: 391 us -> 473 us (1.21)
  blocking collectives: 129 us -> 241 us
  waiting for transfers between devices: 162 us -> 131 us
    all_gather x0 -> x1, blocking collectives: none -> 178 us  [body(): switch_the_indices = lambda point: all_gather(point, TM_DOCS).sum(axis=0)]
    psum x1 -> x0, blocking collectives: 67 us -> none  [body(): totals = lax.psum(placed, TM_DOCS)]
    reduce_scatter x1, waiting for transfers between devices: 22.3 us -> 0.01 us  [body(): lax.psum_scatter((beta_full.astype(jnp.float32) * lax.dot_general(ratios,...]
    all_gather x2, waiting for transfers between devices: 44.2 us -> 36.3 us  [carried_in(): lax.all_gather(part.astype(kind), axis)]
  transfers between devices with their start and end apart: 6 -> 6, of which waited for: 6 -> 5; matrix products, arithmetic and copies ran while one was open for 2% -> 2% of each run, Pallas kernels for 0% -> 0%
where the time goes in v1:
time: 473 us; the launch traced here: 472 us
  blocking collectives  241 us (51%)
  waiting for transfers between devices  131 us (28%)
  matrix products  61.6 us (13%)
  other arithmetic  20.4 us (4%)
  between operations  14.3 us (3%)
    all_gather x1, blocking collectives, body(): switch_the_indices = lambda point: all_gather(point, TM_DOCS).sum(axis=0)  178 us
    all_gather x1, waiting for transfers between devices, body(): beta_full = lax.all_gather(beta_slab, 'docs', axis=0, tiled=True)  51.7 us
    dot_general x4, matrix products, body(): jnp.dot(ratios, beta_full, preferred_element_type=jnp.float32)  45.1 us
    all_gather x2, waiting for transfers between devices, prefix_by_axis(): lax.all_gather(part.astype(kind), axis)  43.4 us
    all_gather x2, blocking collectives, merged(): gathered = jax.tree.map(lambda a: lax.all_gather(a, axis), part)  37.5 us
    all_gather x2, waiting for transfers between devices, carried_in(): lax.all_gather(part.astype(kind), axis)  36.3 us
    all_gather x2, blocking collectives, carried_in(): lax.all_gather(part.astype(kind), axis)  12.5 us
    all_gather x2, blocking collectives, prefix_by_axis(): lax.all_gather(part.astype(kind), axis)  12.5 us
  transfers between devices with their start and end apart: 6, of which 5 were waited for; matrix products, arithmetic and copies ran while one was open for 2% of the time, Pallas kernels for 0%

profile of v1, /device:TPU:1, one launch (start us, length us, event | category | flops | bytes accessed | tf_op | source)
XLA Modules:
  0.0 472.4 jit_solution(16370321237339746659)
XLA Ops:
  7.2 0.0 all-gather.18.cloned.1.call-start
  7.2 1.5 reduce_max.9
  8.7 1.5 fusion.51
  10.2 21.2 %all-gather.6 = f32[16,1,128]{2,1,0:T(1,128)S(1)} all-gather(f32[1,1,128]{2,1,0:T(1,128)S(1)} %bitcast.318), channel_id=2, replica_groups=mesh['tm_0'=4,'tm_1'=2,'docs'=16] {'docs'}, dimensions={0}, use_global_device_ids=true | all-gather | bytes 8704 | tf_op jit(solution)/shard_map/all_gather | solution.py:17
  31.4 16.3 %all-gather.7 = f32[16,1,128]{2,1,0:T(1,128)S(1)} all-gather(f32[1,1,128]{2,1,0:T(1,128)S(1)} %bitcast.319), channel_id=3, replica_groups=mesh['tm_0'=4,'tm_1'=2,'docs'=16] {'docs'}, dimensions={0}, use_global_device_ids=true | all-gather | bytes 8704 | tf_op jit(solution)/shard_map/all_gather | solution.py:17
  47.7 0.7 while.33
  48.4 2.2 fusion.53
  50.5 0.0 all-gather.18.cloned.1.call-update
  50.6 0.0 copy-start.2
  50.6 0.0 reduce-scatter.2.cloned.1.call-start
  50.6 51.7 %all-gather.18.cloned.1.call-done = bf16[32768,128]{1,0:T(8,128)(2,1)} async-done(((bf16[2048,128]{1,0:T(8,128)(2,1)}), bf16[32768,128]{1,0:T(8,128)(2,1)}) %all-gather.18.cloned.1.call-update) | async-done | bytes 8388624 | tf_op jit(solution)/shard_map/all_gather | solution.py:113
  102.3 13.1 %fusion.62 = bf16[64,128]{1,0:T(8,128)(2,1)S(1)} fusion(bf16[32768,128]{1,0:T(8,128)(2,1)} %all-gather.18.cloned.1.call-done, s32[1,64,32768]{2,1,0:T(8,128)} %param.10, f32[1,64,128]{2,1,0:T(8,128)} %param.12, f32[128]{0:T(128)} %param.13), kind=kOutput, calls=%fused_computation.109 | convolution fusion | flops 1081925632 | bytes 16826880 | tf_op jit(solution)/shard_map/dot_general | solution.py:120
  115.4 0.0 copy-done.2
  115.4 12.6 %fusion.66 = bf16[64,128]{1,0:T(8,128)(2,1)S(1)} fusion(bf16[32768,128]{1,0:T(8,128)(2,1)} %all-gather.18.cloned.1.call-done, bf16[64,128]{1,0:T(8,128)(2,1)S(1)} %fusion.62, s32[1,64,32768]{2,1,0:T(8,128)} %param.10, f32[128]{0:T(128)S(1)} %copy-done.2), kind=kOutput, calls=%fused_computation.113 | convolution fusion | flops 1080680448 | bytes 16810496 | tf_op jit(solution)/shard_map/dot_general | solution.py:120
  128.0 12.4 %fusion.15 = f32[64,128]{1,0:T(8,128)S(1)} fusion(bf16[32768,128]{1,0:T(8,128)(2,1)} %all-gather.18.cloned.1.call-done, bf16[64,128]{1,0:T(8,128)(2,1)S(1)} %fusion.66, s32[1,64,32768]{2,1,0:T(8,128)} %param.10, f32[128]{0:T(128)S(1)} %copy-done.2), kind=kOutput, calls=%fused_computation.35 | convolution fusion | flops 1080057856 | bytes 16826880 | tf_op jit(solution)/shard_map/dot_general | solution.py:120
  140.4 9.2 %fusion.3 = bf16[64,32768]{1,0:T(8,128)(2,1)S(1)} fusion(bf16[32768,128]{1,0:T(8,128)(2,1)} %all-gather.18.cloned.1.call-done, s32[1,64,32768]{2,1,0:T(8,128)} %param.10, f32[64,128]{1,0:T(8,128)S(1)} %fusion.15), kind=kOutput, calls=%fused_computation.11 | convolution fusion | flops 543784960 | bytes 21004288 | tf_op jit(solution)/shard_map/dot_general | solution.py:116
  149.6 0.0 copy-start
  149.6 1.9 copy-done
  151.5 7.3 %fusion.2 = bf16[32768,128]{1,0:T(8,128)(2,1)} fusion(bf16[64,32768]{1,0:T(8,128)(2,1)S(1)} %fusion.3, bf16[32768,128]{1,0:T(8,128)(2,1)} %all-gather.18.cloned.1.call-done, f32[64,128]{1,0:T(8,128)S(1)} %fusion.15), kind=kOutput, calls=%fused_computation.9 | convolution fusion | flops 550076416 | bytes 21004288 | tf_op jit(solution)/shard_map/dot_general | solution.py:127
  158.8 0.0 copy-start.1
  158.8 0.0 reduce-scatter.2.cloned.1.call-update
  158.8 0.0 all-gather.24.cloned.1.call-start
  158.9 0.5 copy-done.1
  159.5 0.0 copy-start.3
  159.5 0.0 copy-start.4
  159.5 7.0 %add_bitcast_fusion = (f32[1,64,128]{2,1,0:T(8,128)}, f32[128]{0:T(128)S(1)}) fusion(f32[128]{0:T(128)S(1)} %copy-done.2, bf16[64,32768]{1,0:T(8,128)(2,1)} %copy-done, bf16[32768,128]{1,0:T(8,128)(2,1)} %all-gather.18.cloned.1.call-done, f32[64,128]{1,0:T(8,128)S(1)} %fusion.15), kind=kOutput, calls=%fused_computation.129 | convolution fusion | flops 537526144 | bytes 12649472 | tf_op jit(solution)/shard_map/dot_general | solution.py:120
  166.5 0.1 broadcast_multiply_fusion
  166.6 178.5 %all_gather.60 = f32[128,8,128]{2,1,0:T(8,128)S(1)} all-gather(f32[1,8,128]{2,1,0:T(8,128)S(1)} %broadcast_multiply_fusion), channel_id=1, replica_groups=mesh['tm_0'=4,'tm_1'=2,'docs'=16] {'tm_0','tm_1','docs'}, dimensions={0}, use_global_device_ids=true | all-gather | bytes 528384 | tf_op jit(solution)/shard_map/all_gather | solution.py:139
  345.1 0.2 fusion.309
  345.3 0.0 copy-done.3
  345.3 0.1 divide_multiply_fusion
  345.4 0.8 while.34
  346.2 0.0 copy-done.4
  346.3 0.1 fusion.192
  346.4 0.0 reduce-scatter.2.cloned.1.call-done
  346.4 2.1 fusion.54
  348.5 0.0 all-gather.24.cloned.1.call-update
  348.5 0.0 all-gather.20.cloned.1.call-start
  348.5 4.6 all-gather.10
  353.1 13.7 %all-gather.24.cloned.1.call-done = bf16[4096,128]{1,0:T(8,128)(2,1)} async-done(((bf16[2048,128]{1,0:T(8,128)(2,1)}), bf16[4096,128]{1,0:T(8,128)(2,1)}) %all-gather.24.cloned.1.call-update) | async-done | bytes 1048592 | tf_op jit(solution)/shard_map/all_gather | solution.py:39
  366.9 2.2 fusion.33
  369.1 0.0 all-gather.20.cloned.1.call-update
  369.1 0.0 all-gather.26.cloned.1.call-start
  369.1 7.9 %all-gather.11 = bf16[4,1,128]{2,1,0:T(2,128)(2,1)S(1)} all-gather(bf16[1,1,128]{2,1,0:T(2,128)(2,1)S(1)} %get-tuple-element.217), channel_id=1, replica_groups=mesh['tm_0'=4,'tm_1'=2,'docs'=16] {'tm_0'}, dimensions={0}, use_global_device_ids=true | all-gather | bytes 1280 | tf_op jit(solution)/shard_map/all_gather | solution.py:39
  377.0 22.6 %all-gather.20.cloned.1.call-done = bf16[4,2048,128]{2,1,0:T(8,128)(2,1)} async-done(((bf16[1,2048,128]{2,1,0:T(8,128)(2,1)}), bf16[4,2048,128]{2,1,0:T(8,128)(2,1)}) %all-gather.20.cloned.1.call-update) | async-done | bytes 2097168 | tf_op jit(solution)/shard_map/all_gather | solution.py:39
  399.7 3.9 fusion.310
  403.6 0.0 all-gather.26.cloned.1.call-update
  403.6 0.0 all-gather.22.cloned.1.call-start
  403.7 4.6 all-gather.8
  408.3 20.7 %all-gather.26.cloned.1.call-done = bf16[4096,128]{1,0:T(8,128)(2,1)} async-done(((bf16[2048,128]{1,0:T(8,128)(2,1)}), bf16[4096,128]{1,0:T(8,128)(2,1)}) %all-gather.26.cloned.1.call-update) | async-done | bytes 1048592 | tf_op jit(solution)/shard_map/all_gather | solution.py:60
  429.0 2.2 fusion.37
  431.2 0.0 all-gather.22.cloned.1.call-update
  431.2 7.9 %all-gather.9 = bf16[4,1,128]{2,1,0:T(2,128)(2,1)S(1)} all-gather(bf16[1,1,128]{2,1,0:T(2,128)(2,1)S(1)} %get-tuple-element.213), channel_id=1, replica_groups=mesh['tm_0'=4,'tm_1'=2,'docs'=16] {'tm_0'}, dimensions={0}, use_global_device_ids=true | all-gather | bytes 1280 | tf_op jit(solution)/shard_map/all_gather | solution.py:60
  439.1 22.7 %all-gather.22.cloned.1.call-done = bf16[4,2048,128]{2,1,0:T(8,128)(2,1)} async-done(((bf16[1,2048,128]{2,1,0:T(8,128)(2,1)}), bf16[4,2048,128]{2,1,0:T(8,128)(2,1)}) %all-gather.22.cloned.1.call-update) | async-done | bytes 2097168 | tf_op jit(solution)/shard_map/all_gather | solution.py:60
  461.8 3.7 fusion.24
  (57 shorter events, 1.2 us)
Async XLA Ops:
  7.2 95.1 %all-gather.18.cloned.1.call-start = ((), (), s32[]{:S(2)}) async-start(), calls=%async_computation.1 | async-start | bytes 8912896 | tf_op jit(solution)/shard_map/all_gather | solution.py:113
  50.6 64.9 %copy-start.2 = (f32[128]{0:T(128)S(1)}, f32[128]{0:T(128)}, u32[]{:S(2)}) copy-start(f32[128]{0:T(128)} %param.13) | copy-start | bytes 1540
  50.6 295.8 %reduce-scatter.2.cloned.1.call-start = ((), (), s32[]{:S(2)}) async-start(), calls=%async_computation.2 | async-start | bytes 8912896 | tf_op jit(solution)/shard_map/reduce_scatter | solution.py:124
  149.6 1.9 copy-start
  158.8 0.7 copy-start.1
  158.8 208.0 %all-gather.24.cloned.1.call-start = ((), (), s32[]{:S(2)}) async-start(), calls=%async_computation.5 | async-start | bytes 1572864 | tf_op jit(solution)/shard_map/all_gather | solution.py:39
  159.5 185.8 %copy-start.3 = (f32[128]{0:T(128)S(1)}, f32[128]{0:T(128)}, u32[]{:S(2)}) copy-start(f32[128]{0:T(128)} %param.15) | copy-start | bytes 1540
  159.5 186.8 %copy-start.4 = (pred[8]{0:T(512)(128)(4,1)S(1)}, pred[8]{0:T(512)(128)(4,1)}, u32[]{:S(2)}) copy-start(pred[8]{0:T(512)(128)(4,1)} %constant.117.clone.1) | copy-start | bytes 28
  348.5 51.2 %all-gather.20.cloned.1.call-start = ((), (), s32[]{:S(2)}) async-start(), calls=%async_computation.3 | async-start | bytes 2621440 | tf_op jit(solution)/shard_map/all_gather | solution.py:39
  369.1 59.9 %all-gather.26.cloned.1.call-start = ((), (), s32[]{:S(2)}) async-start(), calls=%async_computation.6 | async-start | bytes 1572864 | tf_op jit(solution)/shard_map/all_gather | solution.py:60
  403.6 58.1 %all-gather.22.cloned.1.call-start = ((), (), s32[]{:S(2)}) async-start(), calls=%async_computation.4 | async-start | bytes 2621440 | tf_op jit(solution)/shard_map/all_gather | solution.py:60
Sparse Core Ops, SparseCore 0:
  50.7 51.5 all-gather.17
  159.0 99.7 reduce-scatter.1
  348.6 18.2 all-gather.23
  369.2 30.4 all-gather.19
  403.8 25.1 all-gather.25
  431.3 30.4 all-gather.21
